TPU v7x, 32 devices: a whole 2x2x4 slice. The times are simulated.
32 devices in a mesh: tm: 2 (over y), space: 16 (over z, x, core).
Axes of the slice: x: 2, y: 2, z: 4, core: 2. Of those that a mesh axis runs over, the one named last changes fastest.
Arguments:
- intensity: float32 [32, 128, 512], P('tm', 'space'), may hold values from 0.05 to 5
- w_first: bfloat16 [3, 3, 48, 32], replicated, may hold values from -0.5 to 0.5
- w_rest: bfloat16 [5, 3, 3, 48, 48], replicated, may hold values from -0.4375 to 0.4375
Outputs:
- front_maps: float32 [48, 128, 512], P(None, 'space', 'tm')
All inputs are finite; a program needn't handle non-finite values.
Results may differ from a plain program's by a relative error of at most 0.03.
Values may be sent and summed in bfloat16 or wider, within the bound.
No kernel may reach another device: no remote copies, remote signals or barrier semaphores. Data moves between devices by JAX's collectives and lax.ppermute only.
A program may use at most 64 MiB of HBM per device.

v0:
```python
import jax
import jax.numpy as jnp
from jax import lax
from jax.sharding import PartitionSpec as P

LAYERS = 6
RADIUS = 3


def extended(x, sides, width):
    for axis, dim in sides:
        size, length = (lax.axis_size(axis), x.shape[dim])
        up = [(i, (i + 1) % size) for i in range(size - 1)]
        down = [(j, i) for i, j in up]
        last = lax.slice_in_dim(x, length - width, length, axis=dim)
        leading = lax.slice_in_dim(x, 0, width, axis=dim)
        before = lax.ppermute(last, axis, up)
        after = lax.ppermute(leading, axis, down)
        x = jnp.concatenate([before, x, after], axis=dim)
    return x


def window_count(start_place, length, overall):
    places = start_place + jnp.arange(length, dtype=jnp.int32)
    upper = jnp.minimum(places + RADIUS, overall - 1)
    lower = jnp.maximum(places - RADIUS, 0)
    return (upper - lower + 1).astype(jnp.float32)


def conv_tile(padded, kernel):
    out_cols = padded.shape[1] - 2
    out_rows = padded.shape[2] - 2
    summed = None
    for a in range(3):
        for b in range(3):
            product = jnp.einsum(
                "oi,ixy->oxy",
                kernel[a, b],
                padded[:, a : a + out_cols, b : b + out_rows],
                preferred_element_type=jnp.float32,
            )
            summed = product if summed is None else summed + product
    return summed


def shards(intensity, w_first, w_rest):
    acq_dev, col_span, row_span = intensity.shape
    space_count = lax.axis_size("space")
    tm_count = lax.axis_size("tm")
    col_start = lax.axis_index("space") * col_span
    widened = extended(intensity, (("space", 1),), RADIUS)
    col_sum = widened[:, 0:col_span, :]
    for k in range(1, 2 * RADIUS + 1):
        col_sum = col_sum + widened[:, k : k + col_span, :]
    row_padded = jnp.pad(col_sum, ((0, 0), (0, 0), (RADIUS, RADIUS)))
    box_sum = row_padded[:, :, 0:row_span]
    for k in range(1, 2 * RADIUS + 1):
        box_sum = box_sum + row_padded[:, :, k : k + row_span]
    cell_count = (
        window_count(col_start, col_span, col_span * space_count)[:, None]
        * window_count(0, row_span, row_span)[None, :]
    )
    local_mean = box_sum / cell_count
    log_mean = jnp.log(local_mean)
    ratio_part = jnp.sum(intensity / local_mean, axis=0)
    acq_total = acq_dev * tm_count
    ratio_sum = lax.psum(ratio_part, "tm")
    features_own = (log_mean + jnp.log(ratio_sum / acq_total)[None]).astype(jnp.bfloat16)
    features = lax.all_to_all(features_own, "tm", split_axis=2, concat_axis=0, tiled=True)
    kernels = [w_first] + [w_rest[k] for k in range(LAYERS - 1)]
    activation = features
    result = None
    for depth_index in range(LAYERS):
        padded = extended(activation, (("tm", 2), ("space", 1)), 1)
        summed = conv_tile(padded, kernels[depth_index])
        if depth_index < LAYERS - 1:
            activation = jnp.maximum(summed, 0.0).astype(jnp.bfloat16)
        else:
            result = summed
    return result


def solution(mesh):
    in_specs = (P("tm", "space", None), P(), P())
    out_specs = P(None, "space", "tm")
    return jax.shard_map(shards, mesh=mesh, in_specs=in_specs, out_specs=out_specs, check_vma=False)
```

profile of v0, /device:TPU:19, one launch (start us, length us, event | category | flops | bytes accessed | tf_op | source)
XLA Modules:
  0.0 145.4 jit_solution(1917381582807719595)
XLA Ops:
  0.0 1.1 fusion.193
  1.1 2.7 %collective-permute-start.1 = (f32[16,3,512]{2,0,1:T(8,128)S(1)}, f32[16,3,512]{2,0,1:T(8,128)S(1)}, u32[]{:S(2)}, u32[]{:S(2)}) collective-permute-start(f32[16,3,512]{2,0,1:T(8,128)S(1)} %copy.56), channel_id=1, source_target_pairs={{1,0},{2,1},{3,2},{4,3},{5,4},{6,5},{7,6},{8,7},{9,8},{10,9},{11,1... | collective-permute-start | bytes 294920 | tf_op jit(solution)/shard_map/ppermute | solution.py:18
  3.9 3.9 %collective-permute-start = (f32[16,3,512]{2,0,1:T(8,128)S(1)}, f32[16,3,512]{2,0,1:T(8,128)S(1)}, u32[]{:S(2)}, u32[]{:S(2)}) collective-permute-start(f32[16,3,512]{2,0,1:T(8,128)S(1)} %copy.55), channel_id=1, source_target_pairs={{0,1},{1,2},{2,3},{3,4},{4,5},{5,6},{6,7},{7,8},{8,9},{9,10},{10,1... | collective-permute-start | bytes 294920 | tf_op jit(solution)/shard_map/ppermute | solution.py:17
  7.9 1.5 %collective-permute-done = f32[16,3,512]{2,0,1:T(8,128)S(1)} collective-permute-done((f32[16,3,512]{2,0,1:T(8,128)S(1)}, f32[16,3,512]{2,0,1:T(8,128)S(1)}, u32[]{:S(2)}, u32[]{:S(2)}) %collective-permute-start) | collective-permute-done | bytes 98336 | tf_op jit(solution)/shard_map/ppermute | solution.py:17
  10.3 6.2 %psum.7 = f32[8,512]{1,0:T(8,128)S(1)} all-reduce(f32[8,512]{1,0:T(8,128)S(1)} %get-tuple-element.5), channel_id=1, replica_groups=mesh['tm'=2,'space'=16] {'tm'}, use_global_device_ids=true, to_apply=%region_1.2 | all-reduce | flops 4096 | bytes 32768 | tf_op jit(solution)/shard_map/psum | solution.py:67
  16.6 0.8 copy.52
  17.4 1.7 %reshape.104 = bf16[2,2,16384]{2,1,0:T(2,128)(2,1)} reshape(bf16[512,8,16]{2,1,0:T(8,128)(2,1)S(1)} %bitcast.310) | data formatting | bytes 262144
  19.1 3.4 %all-to-all-start = ((bf16[2,2,16384]{2,1,0:T(2,128)(2,1)}), bf16[2,2,16384]{2,1,0:T(2,128)(2,1)S(1)}, u32[]{:S(2)}, u32[]{:S(2)}) async-start(bf16[2,2,16384]{2,1,0:T(2,128)(2,1)} %reshape.104), calls=%async_computation | async-start | bytes 262144 | tf_op jit(solution)/shard_map/all_to_all | solution.py:69
  22.6 3.3 %all-to-all-done = bf16[2,2,16384]{2,1,0:T(2,128)(2,1)S(1)} async-done(((bf16[2,2,16384]{2,1,0:T(2,128)(2,1)}), bf16[2,2,16384]{2,1,0:T(2,128)(2,1)S(1)}, u32[]{:S(2)}, u32[]{:S(2)}) %all-to-all-start) | async-done | bytes 131104 | tf_op jit(solution)/shard_map/all_to_all | solution.py:69
  25.8 0.7 reshape.105
  26.5 0.7 copy.53
  27.3 1.9 %collective-permute-start.2 = (bf16[32,8,1]{2,0,1:T(8,128)(2,1)S(1)}, bf16[32,8,1]{2,0,1:T(8,128)(2,1)S(1)}, u32[]{:S(2)}, u32[]{:S(2)}) collective-permute-start(bf16[32,8,1]{2,0,1:T(8,128)(2,1)S(1)} %get-tuple-element.48), channel_id=1, source_target_pairs={{0,16},{1,17},{2,18},{3,19},{4,20},{5,21},{6,22},{7,23},{8,24},{9,... | collective-permute-start | bytes 1544 | tf_op jit(solution)/shard_map/ppermute | solution.py:17
  29.2 1.3 collective-permute-start.3
  30.8 3.4 %collective-permute-done.3 = bf16[32,8,1]{2,0,1:T(8,128)(2,1)S(1)} collective-permute-done((bf16[32,8,1]{2,0,1:T(8,128)(2,1)S(1)}, bf16[32,8,1]{2,0,1:T(8,128)(2,1)S(1)}, u32[]{:S(2)}, u32[]{:S(2)}) %collective-permute-start.3) | collective-permute-done | bytes 544 | tf_op jit(solution)/shard_map/ppermute | solution.py:18
  34.4 9.5 %collective-permute-start.4 = (bf16[32,1,258]{2,0,1:T(8,128)(2,1)S(1)}, bf16[32,1,258]{2,0,1:T(8,128)(2,1)S(1)}, u32[]{:S(2)}, u32[]{:S(2)}) collective-permute-start(bf16[32,1,258]{2,0,1:T(8,128)(2,1)S(1)} %get-tuple-element.34), channel_id=1, source_target_pairs={{0,1},{1,2},{2,3},{3,4},{4,5},{5,6},{6,7},{7,8},{8,9},{9,10},{10,1... | collective-permute-start | bytes 49544 | tf_op jit(solution)/shard_map/ppermute | solution.py:17
  43.9 1.9 %collective-permute-start.5 = (bf16[32,1,258]{2,0,1:T(8,128)(2,1)S(1)}, bf16[32,1,258]{2,0,1:T(8,128)(2,1)S(1)}, u32[]{:S(2)}, u32[]{:S(2)}) collective-permute-start(bf16[32,1,258]{2,0,1:T(8,128)(2,1)S(1)} %get-tuple-element.35), channel_id=1, source_target_pairs={{1,0},{2,1},{3,2},{4,3},{5,4},{6,5},{7,6},{8,7},{9,8},{10,9},{11,1... | collective-permute-start | bytes 49544 | tf_op jit(solution)/shard_map/ppermute | solution.py:18
  46.1 3.8 %collective-permute-done.5 = bf16[32,1,258]{2,0,1:T(8,128)(2,1)S(1)} collective-permute-done((bf16[32,1,258]{2,0,1:T(8,128)(2,1)S(1)}, bf16[32,1,258]{2,0,1:T(8,128)(2,1)S(1)}, u32[]{:S(2)}, u32[]{:S(2)}) %collective-permute-start.5) | collective-permute-done | bytes 16544 | tf_op jit(solution)/shard_map/ppermute | solution.py:18
  52.3 1.3 collective-permute-start.6
  53.6 1.3 collective-permute-start.7
  55.2 3.7 %collective-permute-done.7 = bf16[48,8,1]{2,0,1:T(8,128)(2,1)S(1)} collective-permute-done((bf16[48,8,1]{2,0,1:T(8,128)(2,1)S(1)}, bf16[48,8,1]{2,0,1:T(8,128)(2,1)S(1)}, u32[]{:S(2)}, u32[]{:S(2)}) %collective-permute-start.7) | collective-permute-done | bytes 800 | tf_op jit(solution)/shard_map/ppermute | solution.py:18
  59.0 3.4 %collective-permute-start.8 = (bf16[48,1,258]{2,0,1:T(8,128)(2,1)S(1)}, bf16[48,1,258]{2,0,1:T(8,128)(2,1)S(1)}, u32[]{:S(2)}, u32[]{:S(2)}) collective-permute-start(bf16[48,1,258]{2,0,1:T(8,128)(2,1)S(1)} %get-tuple-element.30), channel_id=1, source_target_pairs={{0,1},{1,2},{2,3},{3,4},{4,5},{5,6},{6,7},{7,8},{8,9},{9,10},{10,1... | collective-permute-start | bytes 74312 | tf_op jit(solution)/shard_map/ppermute | solution.py:17
  62.4 1.9 %collective-permute-start.9 = (bf16[48,1,258]{2,0,1:T(8,128)(2,1)S(1)}, bf16[48,1,258]{2,0,1:T(8,128)(2,1)S(1)}, u32[]{:S(2)}, u32[]{:S(2)}) collective-permute-start(bf16[48,1,258]{2,0,1:T(8,128)(2,1)S(1)} %get-tuple-element.31), channel_id=1, source_target_pairs={{1,0},{2,1},{3,2},{4,3},{5,4},{6,5},{7,6},{8,7},{9,8},{10,9},{11,1... | collective-permute-start | bytes 74312 | tf_op jit(solution)/shard_map/ppermute | solution.py:18
  64.6 4.0 %collective-permute-done.9 = bf16[48,1,258]{2,0,1:T(8,128)(2,1)S(1)} collective-permute-done((bf16[48,1,258]{2,0,1:T(8,128)(2,1)S(1)}, bf16[48,1,258]{2,0,1:T(8,128)(2,1)S(1)}, u32[]{:S(2)}, u32[]{:S(2)}) %collective-permute-start.9) | collective-permute-done | bytes 24800 | tf_op jit(solution)/shard_map/ppermute | solution.py:18
  70.8 1.3 collective-permute-start.10
  72.1 1.3 collective-permute-start.11
  73.7 3.7 %collective-permute-done.11 = bf16[48,8,1]{2,0,1:T(8,128)(2,1)S(1)} collective-permute-done((bf16[48,8,1]{2,0,1:T(8,128)(2,1)S(1)}, bf16[48,8,1]{2,0,1:T(8,128)(2,1)S(1)}, u32[]{:S(2)}, u32[]{:S(2)}) %collective-permute-start.11) | collective-permute-done | bytes 800 | tf_op jit(solution)/shard_map/ppermute | solution.py:18
  77.5 3.3 %collective-permute-start.12 = (bf16[48,1,258]{2,0,1:T(8,128)(2,1)S(1)}, bf16[48,1,258]{2,0,1:T(8,128)(2,1)S(1)}, u32[]{:S(2)}, u32[]{:S(2)}) collective-permute-start(bf16[48,1,258]{2,0,1:T(8,128)(2,1)S(1)} %get-tuple-element.26), channel_id=1, source_target_pairs={{0,1},{1,2},{2,3},{3,4},{4,5},{5,6},{6,7},{7,8},{8,9},{9,10},{10,1... | collective-permute-start | bytes 74312 | tf_op jit(solution)/shard_map/ppermute | solution.py:17
  80.8 1.9 %collective-permute-start.13 = (bf16[48,1,258]{2,0,1:T(8,128)(2,1)S(1)}, bf16[48,1,258]{2,0,1:T(8,128)(2,1)S(1)}, u32[]{:S(2)}, u32[]{:S(2)}) collective-permute-start(bf16[48,1,258]{2,0,1:T(8,128)(2,1)S(1)} %get-tuple-element.27), channel_id=1, source_target_pairs={{1,0},{2,1},{3,2},{4,3},{5,4},{6,5},{7,6},{8,7},{9,8},{10,9},{11,1... | collective-permute-start | bytes 74312 | tf_op jit(solution)/shard_map/ppermute | solution.py:18
  83.0 4.0 %collective-permute-done.13 = bf16[48,1,258]{2,0,1:T(8,128)(2,1)S(1)} collective-permute-done((bf16[48,1,258]{2,0,1:T(8,128)(2,1)S(1)}, bf16[48,1,258]{2,0,1:T(8,128)(2,1)S(1)}, u32[]{:S(2)}, u32[]{:S(2)}) %collective-permute-start.13) | collective-permute-done | bytes 24800 | tf_op jit(solution)/shard_map/ppermute | solution.py:18
  89.2 1.3 collective-permute-start.14
  90.5 1.3 collective-permute-start.15
  92.1 3.7 %collective-permute-done.15 = bf16[48,8,1]{2,0,1:T(8,128)(2,1)S(1)} collective-permute-done((bf16[48,8,1]{2,0,1:T(8,128)(2,1)S(1)}, bf16[48,8,1]{2,0,1:T(8,128)(2,1)S(1)}, u32[]{:S(2)}, u32[]{:S(2)}) %collective-permute-start.15) | collective-permute-done | bytes 800 | tf_op jit(solution)/shard_map/ppermute | solution.py:18
  96.0 3.3 %collective-permute-start.16 = (bf16[48,1,258]{2,0,1:T(8,128)(2,1)S(1)}, bf16[48,1,258]{2,0,1:T(8,128)(2,1)S(1)}, u32[]{:S(2)}, u32[]{:S(2)}) collective-permute-start(bf16[48,1,258]{2,0,1:T(8,128)(2,1)S(1)} %get-tuple-element.22), channel_id=1, source_target_pairs={{0,1},{1,2},{2,3},{3,4},{4,5},{5,6},{6,7},{7,8},{8,9},{9,10},{10,1... | collective-permute-start | bytes 74312 | tf_op jit(solution)/shard_map/ppermute | solution.py:17
  99.3 2.1 %collective-permute-start.17 = (bf16[48,1,258]{2,0,1:T(8,128)(2,1)S(1)}, bf16[48,1,258]{2,0,1:T(8,128)(2,1)S(1)}, u32[]{:S(2)}, u32[]{:S(2)}) collective-permute-start(bf16[48,1,258]{2,0,1:T(8,128)(2,1)S(1)} %get-tuple-element.23), channel_id=1, source_target_pairs={{1,0},{2,1},{3,2},{4,3},{5,4},{6,5},{7,6},{8,7},{9,8},{10,9},{11,1... | collective-permute-start | bytes 74312 | tf_op jit(solution)/shard_map/ppermute | solution.py:18
  101.7 3.8 %collective-permute-done.17 = bf16[48,1,258]{2,0,1:T(8,128)(2,1)S(1)} collective-permute-done((bf16[48,1,258]{2,0,1:T(8,128)(2,1)S(1)}, bf16[48,1,258]{2,0,1:T(8,128)(2,1)S(1)}, u32[]{:S(2)}, u32[]{:S(2)}) %collective-permute-start.17) | collective-permute-done | bytes 24800 | tf_op jit(solution)/shard_map/ppermute | solution.py:18
  107.6 1.3 collective-permute-start.18
  109.0 1.3 collective-permute-start.19
  110.6 3.7 %collective-permute-done.19 = bf16[48,8,1]{2,0,1:T(8,128)(2,1)S(1)} collective-permute-done((bf16[48,8,1]{2,0,1:T(8,128)(2,1)S(1)}, bf16[48,8,1]{2,0,1:T(8,128)(2,1)S(1)}, u32[]{:S(2)}, u32[]{:S(2)}) %collective-permute-start.19) | collective-permute-done | bytes 800 | tf_op jit(solution)/shard_map/ppermute | solution.py:18
  114.4 3.3 %collective-permute-start.20 = (bf16[48,1,258]{2,0,1:T(8,128)(2,1)S(1)}, bf16[48,1,258]{2,0,1:T(8,128)(2,1)S(1)}, u32[]{:S(2)}, u32[]{:S(2)}) collective-permute-start(bf16[48,1,258]{2,0,1:T(8,128)(2,1)S(1)} %get-tuple-element.18), channel_id=1, source_target_pairs={{0,1},{1,2},{2,3},{3,4},{4,5},{5,6},{6,7},{7,8},{8,9},{9,10},{10,1... | collective-permute-start | bytes 74312 | tf_op jit(solution)/shard_map/ppermute | solution.py:17
  117.7 1.9 %collective-permute-start.21 = (bf16[48,1,258]{2,0,1:T(8,128)(2,1)S(1)}, bf16[48,1,258]{2,0,1:T(8,128)(2,1)S(1)}, u32[]{:S(2)}, u32[]{:S(2)}) collective-permute-start(bf16[48,1,258]{2,0,1:T(8,128)(2,1)S(1)} %get-tuple-element.19), channel_id=1, source_target_pairs={{1,0},{2,1},{3,2},{4,3},{5,4},{6,5},{7,6},{8,7},{9,8},{10,9},{11,1... | collective-permute-start | bytes 74312 | tf_op jit(solution)/shard_map/ppermute | solution.py:18
  119.9 4.0 %collective-permute-done.21 = bf16[48,1,258]{2,0,1:T(8,128)(2,1)S(1)} collective-permute-done((bf16[48,1,258]{2,0,1:T(8,128)(2,1)S(1)}, bf16[48,1,258]{2,0,1:T(8,128)(2,1)S(1)}, u32[]{:S(2)}, u32[]{:S(2)}) %collective-permute-start.21) | collective-permute-done | bytes 24800 | tf_op jit(solution)/shard_map/ppermute | solution.py:18
  126.1 1.3 collective-permute-start.22
  127.4 1.3 collective-permute-start.23
  129.0 3.7 %collective-permute-done.23 = bf16[48,8,1]{2,0,1:T(8,128)(2,1)S(1)} collective-permute-done((bf16[48,8,1]{2,0,1:T(8,128)(2,1)S(1)}, bf16[48,8,1]{2,0,1:T(8,128)(2,1)S(1)}, u32[]{:S(2)}, u32[]{:S(2)}) %collective-permute-start.23) | collective-permute-done | bytes 800 | tf_op jit(solution)/shard_map/ppermute | solution.py:18
  132.8 3.3 %collective-permute-start.24 = (bf16[48,1,258]{2,0,1:T(8,128)(2,1)S(1)}, bf16[48,1,258]{2,0,1:T(8,128)(2,1)S(1)}, u32[]{:S(2)}, u32[]{:S(2)}) collective-permute-start(bf16[48,1,258]{2,0,1:T(8,128)(2,1)S(1)} %get-tuple-element.14), channel_id=1, source_target_pairs={{0,1},{1,2},{2,3},{3,4},{4,5},{5,6},{6,7},{7,8},{8,9},{9,10},{10,1... | collective-permute-start | bytes 74312 | tf_op jit(solution)/shard_map/ppermute | solution.py:17
  136.1 1.9 %collective-permute-start.25 = (bf16[48,1,258]{2,0,1:T(8,128)(2,1)S(1)}, bf16[48,1,258]{2,0,1:T(8,128)(2,1)S(1)}, u32[]{:S(2)}, u32[]{:S(2)}) collective-permute-start(bf16[48,1,258]{2,0,1:T(8,128)(2,1)S(1)} %get-tuple-element.15), channel_id=1, source_target_pairs={{1,0},{2,1},{3,2},{4,3},{5,4},{6,5},{7,6},{8,7},{9,8},{10,9},{11,1... | collective-permute-start | bytes 74312 | tf_op jit(solution)/shard_map/ppermute | solution.py:18
  138.3 4.0 %collective-permute-done.25 = bf16[48,1,258]{2,0,1:T(8,128)(2,1)S(1)} collective-permute-done((bf16[48,1,258]{2,0,1:T(8,128)(2,1)S(1)}, bf16[48,1,258]{2,0,1:T(8,128)(2,1)S(1)}, u32[]{:S(2)}, u32[]{:S(2)}) %collective-permute-start.25) | collective-permute-done | bytes 24800 | tf_op jit(solution)/shard_map/ppermute | solution.py:18
  144.4 1.0 copy.54
  (104 shorter events, 18.1 us)
Async XLA Ops:
  1.1 6.8 %copy-start = (f32[16,8,512]{2,1,0:T(8,128)S(1)}, f32[16,8,512]{2,1,0:T(8,128)}, u32[]{:S(2)}) copy-start(f32[16,8,512]{2,1,0:T(8,128)} %param.3) | copy-start | bytes 786436
  1.1 8.3 %collective-permute-start.1 = (f32[16,3,512]{2,0,1:T(8,128)S(1)}, f32[16,3,512]{2,0,1:T(8,128)S(1)}, u32[]{:S(2)}, u32[]{:S(2)}) collective-permute-start(f32[16,3,512]{2,0,1:T(8,128)S(1)} %copy.56), channel_id=1, source_target_pairs={{1,0},{2,1},{3,2},{4,3},{5,4},{6,5},{7,6},{8,7},{9,8},{10,9},{11,1... | collective-permute-start | bytes 294920 | tf_op jit(solution)/shard_map/ppermute | solution.py:18
  3.9 5.5 %collective-permute-start = (f32[16,3,512]{2,0,1:T(8,128)S(1)}, f32[16,3,512]{2,0,1:T(8,128)S(1)}, u32[]{:S(2)}, u32[]{:S(2)}) collective-permute-start(f32[16,3,512]{2,0,1:T(8,128)S(1)} %copy.55), channel_id=1, source_target_pairs={{0,1},{1,2},{2,3},{3,4},{4,5},{5,6},{6,7},{7,8},{8,9},{9,10},{10,1... | collective-permute-start | bytes 294920 | tf_op jit(solution)/shard_map/ppermute | solution.py:17
  17.4 5.1 %copy-start.1 = (bf16[5,3,3,48,48]{4,3,2,1,0:T(8,128)(2,1)S(1)}, bf16[5,3,3,48,48]{4,3,2,1,0:T(8,128)(2,1)}, u32[]{:S(2)}) copy-start(bf16[5,3,3,48,48]{4,3,2,1,0:T(8,128)(2,1)} %param.5) | copy-start | bytes 622084
  19.1 6.7 %all-to-all-start = ((bf16[2,2,16384]{2,1,0:T(2,128)(2,1)}), bf16[2,2,16384]{2,1,0:T(2,128)(2,1)S(1)}, u32[]{:S(2)}, u32[]{:S(2)}) async-start(bf16[2,2,16384]{2,1,0:T(2,128)(2,1)} %reshape.104), calls=%async_computation | async-start | bytes 262144 | tf_op jit(solution)/shard_map/all_to_all | solution.py:69
  27.2 3.3 %copy-start.2 = (bf16[3,3,48,32]{2,3,1,0:T(8,128)(2,1)S(1)}, bf16[3,3,48,32]{2,3,1,0:T(8,128)(2,1)}, u32[]{:S(2)}) copy-start(bf16[3,3,48,32]{2,3,1,0:T(8,128)(2,1)} %param.4) | copy-start | bytes 82948
  27.3 3.5 %collective-permute-start.2 = (bf16[32,8,1]{2,0,1:T(8,128)(2,1)S(1)}, bf16[32,8,1]{2,0,1:T(8,128)(2,1)S(1)}, u32[]{:S(2)}, u32[]{:S(2)}) collective-permute-start(bf16[32,8,1]{2,0,1:T(8,128)(2,1)S(1)} %get-tuple-element.48), channel_id=1, source_target_pairs={{0,16},{1,17},{2,18},{3,19},{4,20},{5,21},{6,22},{7,23},{8,24},{9,... | collective-permute-start | bytes 1544 | tf_op jit(solution)/shard_map/ppermute | solution.py:17
  29.2 5.0 %collective-permute-start.3 = (bf16[32,8,1]{2,0,1:T(8,128)(2,1)S(1)}, bf16[32,8,1]{2,0,1:T(8,128)(2,1)S(1)}, u32[]{:S(2)}, u32[]{:S(2)}) collective-permute-start(bf16[32,8,1]{2,0,1:T(8,128)(2,1)S(1)} %get-tuple-element.49), channel_id=1, source_target_pairs={{16,0},{17,1},{18,2},{19,3},{20,4},{21,5},{22,6},{23,7},{24,8},{25... | collective-permute-start | bytes 1544 | tf_op jit(solution)/shard_map/ppermute | solution.py:18
  34.4 11.8 %collective-permute-start.4 = (bf16[32,1,258]{2,0,1:T(8,128)(2,1)S(1)}, bf16[32,1,258]{2,0,1:T(8,128)(2,1)S(1)}, u32[]{:S(2)}, u32[]{:S(2)}) collective-permute-start(bf16[32,1,258]{2,0,1:T(8,128)(2,1)S(1)} %get-tuple-element.34), channel_id=1, source_target_pairs={{0,1},{1,2},{2,3},{3,4},{4,5},{5,6},{6,7},{7,8},{8,9},{9,10},{10,1... | collective-permute-start | bytes 49544 | tf_op jit(solution)/shard_map/ppermute | solution.py:17
  43.9 6.0 %collective-permute-start.5 = (bf16[32,1,258]{2,0,1:T(8,128)(2,1)S(1)}, bf16[32,1,258]{2,0,1:T(8,128)(2,1)S(1)}, u32[]{:S(2)}, u32[]{:S(2)}) collective-permute-start(bf16[32,1,258]{2,0,1:T(8,128)(2,1)S(1)} %get-tuple-element.35), channel_id=1, source_target_pairs={{1,0},{2,1},{3,2},{4,3},{5,4},{6,5},{7,6},{8,7},{9,8},{10,9},{11,1... | collective-permute-start | bytes 49544 | tf_op jit(solution)/shard_map/ppermute | solution.py:18
  52.3 2.9 %collective-permute-start.6 = (bf16[48,8,1]{2,0,1:T(8,128)(2,1)S(1)}, bf16[48,8,1]{2,0,1:T(8,128)(2,1)S(1)}, u32[]{:S(2)}, u32[]{:S(2)}) collective-permute-start(bf16[48,8,1]{2,0,1:T(8,128)(2,1)S(1)} %get-tuple-element.46), channel_id=1, source_target_pairs={{0,16},{1,17},{2,18},{3,19},{4,20},{5,21},{6,22},{7,23},{8,24},{9,... | collective-permute-start | bytes 2312 | tf_op jit(solution)/shard_map/ppermute | solution.py:17
  53.6 5.4 %collective-permute-start.7 = (bf16[48,8,1]{2,0,1:T(8,128)(2,1)S(1)}, bf16[48,8,1]{2,0,1:T(8,128)(2,1)S(1)}, u32[]{:S(2)}, u32[]{:S(2)}) collective-permute-start(bf16[48,8,1]{2,0,1:T(8,128)(2,1)S(1)} %get-tuple-element.47), channel_id=1, source_target_pairs={{16,0},{17,1},{18,2},{19,3},{20,4},{21,5},{22,6},{23,7},{24,8},{25... | collective-permute-start | bytes 2312 | tf_op jit(solution)/shard_map/ppermute | solution.py:18
  59.0 5.6 %collective-permute-start.8 = (bf16[48,1,258]{2,0,1:T(8,128)(2,1)S(1)}, bf16[48,1,258]{2,0,1:T(8,128)(2,1)S(1)}, u32[]{:S(2)}, u32[]{:S(2)}) collective-permute-start(bf16[48,1,258]{2,0,1:T(8,128)(2,1)S(1)} %get-tuple-element.30), channel_id=1, source_target_pairs={{0,1},{1,2},{2,3},{3,4},{4,5},{5,6},{6,7},{7,8},{8,9},{9,10},{10,1... | collective-permute-start | bytes 74312 | tf_op jit(solution)/shard_map/ppermute | solution.py:17
  62.4 6.2 %collective-permute-start.9 = (bf16[48,1,258]{2,0,1:T(8,128)(2,1)S(1)}, bf16[48,1,258]{2,0,1:T(8,128)(2,1)S(1)}, u32[]{:S(2)}, u32[]{:S(2)}) collective-permute-start(bf16[48,1,258]{2,0,1:T(8,128)(2,1)S(1)} %get-tuple-element.31), channel_id=1, source_target_pairs={{1,0},{2,1},{3,2},{4,3},{5,4},{6,5},{7,6},{8,7},{9,8},{10,9},{11,1... | collective-permute-start | bytes 74312 | tf_op jit(solution)/shard_map/ppermute | solution.py:18
  70.8 2.9 %collective-permute-start.10 = (bf16[48,8,1]{2,0,1:T(8,128)(2,1)S(1)}, bf16[48,8,1]{2,0,1:T(8,128)(2,1)S(1)}, u32[]{:S(2)}, u32[]{:S(2)}) collective-permute-start(bf16[48,8,1]{2,0,1:T(8,128)(2,1)S(1)} %get-tuple-element.44), channel_id=1, source_target_pairs={{0,16},{1,17},{2,18},{3,19},{4,20},{5,21},{6,22},{7,23},{8,24},{9,... | collective-permute-start | bytes 2312 | tf_op jit(solution)/shard_map/ppermute | solution.py:17
  72.1 5.4 %collective-permute-start.11 = (bf16[48,8,1]{2,0,1:T(8,128)(2,1)S(1)}, bf16[48,8,1]{2,0,1:T(8,128)(2,1)S(1)}, u32[]{:S(2)}, u32[]{:S(2)}) collective-permute-start(bf16[48,8,1]{2,0,1:T(8,128)(2,1)S(1)} %get-tuple-element.45), channel_id=1, source_target_pairs={{16,0},{17,1},{18,2},{19,3},{20,4},{21,5},{22,6},{23,7},{24,8},{25... | collective-permute-start | bytes 2312 | tf_op jit(solution)/shard_map/ppermute | solution.py:18
  77.5 5.5 %collective-permute-start.12 = (bf16[48,1,258]{2,0,1:T(8,128)(2,1)S(1)}, bf16[48,1,258]{2,0,1:T(8,128)(2,1)S(1)}, u32[]{:S(2)}, u32[]{:S(2)}) collective-permute-start(bf16[48,1,258]{2,0,1:T(8,128)(2,1)S(1)} %get-tuple-element.26), channel_id=1, source_target_pairs={{0,1},{1,2},{2,3},{3,4},{4,5},{5,6},{6,7},{7,8},{8,9},{9,10},{10,1... | collective-permute-start | bytes 74312 | tf_op jit(solution)/shard_map/ppermute | solution.py:17
  80.8 6.2 %collective-permute-start.13 = (bf16[48,1,258]{2,0,1:T(8,128)(2,1)S(1)}, bf16[48,1,258]{2,0,1:T(8,128)(2,1)S(1)}, u32[]{:S(2)}, u32[]{:S(2)}) collective-permute-start(bf16[48,1,258]{2,0,1:T(8,128)(2,1)S(1)} %get-tuple-element.27), channel_id=1, source_target_pairs={{1,0},{2,1},{3,2},{4,3},{5,4},{6,5},{7,6},{8,7},{9,8},{10,9},{11,1... | collective-permute-start | bytes 74312 | tf_op jit(solution)/shard_map/ppermute | solution.py:18
  89.2 2.9 %collective-permute-start.14 = (bf16[48,8,1]{2,0,1:T(8,128)(2,1)S(1)}, bf16[48,8,1]{2,0,1:T(8,128)(2,1)S(1)}, u32[]{:S(2)}, u32[]{:S(2)}) collective-permute-start(bf16[48,8,1]{2,0,1:T(8,128)(2,1)S(1)} %get-tuple-element.42), channel_id=1, source_target_pairs={{0,16},{1,17},{2,18},{3,19},{4,20},{5,21},{6,22},{7,23},{8,24},{9,... | collective-permute-start | bytes 2312 | tf_op jit(solution)/shard_map/ppermute | solution.py:17
  90.5 5.4 %collective-permute-start.15 = (bf16[48,8,1]{2,0,1:T(8,128)(2,1)S(1)}, bf16[48,8,1]{2,0,1:T(8,128)(2,1)S(1)}, u32[]{:S(2)}, u32[]{:S(2)}) collective-permute-start(bf16[48,8,1]{2,0,1:T(8,128)(2,1)S(1)} %get-tuple-element.43), channel_id=1, source_target_pairs={{16,0},{17,1},{18,2},{19,3},{20,4},{21,5},{22,6},{23,7},{24,8},{25... | collective-permute-start | bytes 2312 | tf_op jit(solution)/shard_map/ppermute | solution.py:18
  96.0 5.7 %collective-permute-start.16 = (bf16[48,1,258]{2,0,1:T(8,128)(2,1)S(1)}, bf16[48,1,258]{2,0,1:T(8,128)(2,1)S(1)}, u32[]{:S(2)}, u32[]{:S(2)}) collective-permute-start(bf16[48,1,258]{2,0,1:T(8,128)(2,1)S(1)} %get-tuple-element.22), channel_id=1, source_target_pairs={{0,1},{1,2},{2,3},{3,4},{4,5},{5,6},{6,7},{7,8},{8,9},{9,10},{10,1... | collective-permute-start | bytes 74312 | tf_op jit(solution)/shard_map/ppermute | solution.py:17
  99.3 6.2 %collective-permute-start.17 = (bf16[48,1,258]{2,0,1:T(8,128)(2,1)S(1)}, bf16[48,1,258]{2,0,1:T(8,128)(2,1)S(1)}, u32[]{:S(2)}, u32[]{:S(2)}) collective-permute-start(bf16[48,1,258]{2,0,1:T(8,128)(2,1)S(1)} %get-tuple-element.23), channel_id=1, source_target_pairs={{1,0},{2,1},{3,2},{4,3},{5,4},{6,5},{7,6},{8,7},{9,8},{10,9},{11,1... | collective-permute-start | bytes 74312 | tf_op jit(solution)/shard_map/ppermute | solution.py:18
  107.6 2.9 %collective-permute-start.18 = (bf16[48,8,1]{2,0,1:T(8,128)(2,1)S(1)}, bf16[48,8,1]{2,0,1:T(8,128)(2,1)S(1)}, u32[]{:S(2)}, u32[]{:S(2)}) collective-permute-start(bf16[48,8,1]{2,0,1:T(8,128)(2,1)S(1)} %get-tuple-element.40), channel_id=1, source_target_pairs={{0,16},{1,17},{2,18},{3,19},{4,20},{5,21},{6,22},{7,23},{8,24},{9,... | collective-permute-start | bytes 2312 | tf_op jit(solution)/shard_map/ppermute | solution.py:17
  109.0 5.4 %collective-permute-start.19 = (bf16[48,8,1]{2,0,1:T(8,128)(2,1)S(1)}, bf16[48,8,1]{2,0,1:T(8,128)(2,1)S(1)}, u32[]{:S(2)}, u32[]{:S(2)}) collective-permute-start(bf16[48,8,1]{2,0,1:T(8,128)(2,1)S(1)} %get-tuple-element.41), channel_id=1, source_target_pairs={{16,0},{17,1},{18,2},{19,3},{20,4},{21,5},{22,6},{23,7},{24,8},{25... | collective-permute-start | bytes 2312 | tf_op jit(solution)/shard_map/ppermute | solution.py:18
  114.4 5.5 %collective-permute-start.20 = (bf16[48,1,258]{2,0,1:T(8,128)(2,1)S(1)}, bf16[48,1,258]{2,0,1:T(8,128)(2,1)S(1)}, u32[]{:S(2)}, u32[]{:S(2)}) collective-permute-start(bf16[48,1,258]{2,0,1:T(8,128)(2,1)S(1)} %get-tuple-element.18), channel_id=1, source_target_pairs={{0,1},{1,2},{2,3},{3,4},{4,5},{5,6},{6,7},{7,8},{8,9},{9,10},{10,1... | collective-permute-start | bytes 74312 | tf_op jit(solution)/shard_map/ppermute | solution.py:17
  117.7 6.2 %collective-permute-start.21 = (bf16[48,1,258]{2,0,1:T(8,128)(2,1)S(1)}, bf16[48,1,258]{2,0,1:T(8,128)(2,1)S(1)}, u32[]{:S(2)}, u32[]{:S(2)}) collective-permute-start(bf16[48,1,258]{2,0,1:T(8,128)(2,1)S(1)} %get-tuple-element.19), channel_id=1, source_target_pairs={{1,0},{2,1},{3,2},{4,3},{5,4},{6,5},{7,6},{8,7},{9,8},{10,9},{11,1... | collective-permute-start | bytes 74312 | tf_op jit(solution)/shard_map/ppermute | solution.py:18
  126.1 2.9 %collective-permute-start.22 = (bf16[48,8,1]{2,0,1:T(8,128)(2,1)S(1)}, bf16[48,8,1]{2,0,1:T(8,128)(2,1)S(1)}, u32[]{:S(2)}, u32[]{:S(2)}) collective-permute-start(bf16[48,8,1]{2,0,1:T(8,128)(2,1)S(1)} %get-tuple-element.38), channel_id=1, source_target_pairs={{0,16},{1,17},{2,18},{3,19},{4,20},{5,21},{6,22},{7,23},{8,24},{9,... | collective-permute-start | bytes 2312 | tf_op jit(solution)/shard_map/ppermute | solution.py:17
  127.4 5.4 %collective-permute-start.23 = (bf16[48,8,1]{2,0,1:T(8,128)(2,1)S(1)}, bf16[48,8,1]{2,0,1:T(8,128)(2,1)S(1)}, u32[]{:S(2)}, u32[]{:S(2)}) collective-permute-start(bf16[48,8,1]{2,0,1:T(8,128)(2,1)S(1)} %get-tuple-element.39), channel_id=1, source_target_pairs={{16,0},{17,1},{18,2},{19,3},{20,4},{21,5},{22,6},{23,7},{24,8},{25... | collective-permute-start | bytes 2312 | tf_op jit(solution)/shard_map/ppermute | solution.py:18
  132.8 5.5 %collective-permute-start.24 = (bf16[48,1,258]{2,0,1:T(8,128)(2,1)S(1)}, bf16[48,1,258]{2,0,1:T(8,128)(2,1)S(1)}, u32[]{:S(2)}, u32[]{:S(2)}) collective-permute-start(bf16[48,1,258]{2,0,1:T(8,128)(2,1)S(1)} %get-tuple-element.14), channel_id=1, source_target_pairs={{0,1},{1,2},{2,3},{3,4},{4,5},{5,6},{6,7},{7,8},{8,9},{9,10},{10,1... | collective-permute-start | bytes 74312 | tf_op jit(solution)/shard_map/ppermute | solution.py:17
  136.1 6.2 %collective-permute-start.25 = (bf16[48,1,258]{2,0,1:T(8,128)(2,1)S(1)}, bf16[48,1,258]{2,0,1:T(8,128)(2,1)S(1)}, u32[]{:S(2)}, u32[]{:S(2)}) collective-permute-start(bf16[48,1,258]{2,0,1:T(8,128)(2,1)S(1)} %get-tuple-element.15), channel_id=1, source_target_pairs={{1,0},{2,1},{3,2},{4,3},{5,4},{6,5},{7,6},{8,7},{9,8},{10,9},{11,1... | collective-permute-start | bytes 74312 | tf_op jit(solution)/shard_map/ppermute | solution.py:18
where the time goes:
time: 146 us; the launch traced here: 145 us
  starting transfers between devices  63.9 us (44%)
  waiting for transfers between devices  51.1 us (35%)
  matrix products  13.4 us (9%)
  local copies, waits for them, and re-layouts  6.89 us (5%)
  blocking collectives  6.17 us (4%)
  other arithmetic  3.07 us (2%)
    ppermute x13, waiting for transfers between devices, extended(): after = lax.ppermute(leading, axis, down)  45.7 us
    ppermute x13, starting transfers between devices, extended(): before = lax.ppermute(last, axis, up)  38.3 us
    ppermute x13, starting transfers between devices, extended(): after = lax.ppermute(leading, axis, down)  22.2 us
    dot_general x54, matrix products, conv_tile(): jnp.einsum('oi,ixy->oxy', kernel[a, b], padded[:, a:a + out_cols, b:b + o...  13.4 us
    psum x1, blocking collectives, shards(): ratio_sum = lax.psum(ratio_part, 'tm')  6.17 us
    all_to_all x1, starting transfers between devices, shards(): lax.all_to_all(features_own, 'tm', split_axis=2, concat_axis=0, tiled=True)  3.38 us
    all_to_all x1, waiting for transfers between devices, shards(): lax.all_to_all(features_own, 'tm', split_axis=2, concat_axis=0, tiled=True)  3.25 us
  transfers between devices with their start and end apart: 27, of which 19 were waited for; matrix products, arithmetic and copies ran while one was open for 2% of the time, Pallas kernels for 0%

commit v1 on v0

--- a/solution.py
+++ b/solution.py
@@ -66,7 +66,10 @@
     acq_total = acq_dev * tm_count
     ratio_sum = lax.psum(ratio_part, "tm")
     features_own = (log_mean + jnp.log(ratio_sum / acq_total)[None]).astype(jnp.bfloat16)
-    features = lax.all_to_all(features_own, "tm", split_axis=2, concat_axis=0, tiled=True)
+    features = jnp.concatenate(
+        lax.all_to_all(jnp.stack(jnp.split(features_own, lax.axis_size("tm"), axis=2)), "tm", 0, 0),
+        axis=0,
+    )
     kernels = [w_first] + [w_rest[k] for k in range(LAYERS - 1)]
     activation = features
     result = None

time: 146 us -> 144 us (0.986)
  local copies, waits for them, and re-layouts: 6.89 us -> 2.87 us
    unnamed x11 -> x7, local copies, waits for them, and re-layouts: 2.53 us -> 0.03 us
  transfers between devices with their start and end apart: 27 -> 27, of which waited for: 19 -> 20; matrix products, arithmetic and copies ran while one was open for 2% -> 2% of each run, Pallas kernels for 0% -> 0%
where the time goes in v1:
time: 144 us; the launch traced here: 143 us
  starting transfers between devices  64.2 us (45%)
  waiting for transfers between devices  51.5 us (36%)
  matrix products  13.4 us (9%)
  blocking collectives  6.17 us (4%)
  other arithmetic  3.73 us (3%)
  local copies, waits for them, and re-layouts  2.87 us (2%)
    ppermute x13, waiting for transfers between devices, extended(): after = lax.ppermute(leading, axis, down)  46.4 us
    ppermute x13, starting transfers between devices, extended(): before = lax.ppermute(last, axis, up)  39 us
    ppermute x13, starting transfers between devices, extended(): after = lax.ppermute(leading, axis, down)  21.9 us
    dot_general x54, matrix products, conv_tile(): jnp.einsum('oi,ixy->oxy', kernel[a, b], padded[:, a:a + out_cols, b:b + o...  13.4 us
    psum x1, blocking collectives, shards(): ratio_sum = lax.psum(ratio_part, 'tm')  6.17 us
    all_to_all x1, starting transfers between devices, shards(): lax.all_to_all(jnp.stack(jnp.split(features_own, lax.axis_size('tm'), axi...  3.38 us
    all_to_all x1, waiting for transfers between devices, shards(): lax.all_to_all(jnp.stack(jnp.split(features_own, lax.axis_size('tm'), axi...  3.25 us
  transfers between devices with their start and end apart: 27, of which 20 were waited for; matrix products, arithmetic and copies ran while one was open for 2% of the time, Pallas kernels for 0%

profile of v1, /device:TPU:19, one launch (start us, length us, event | category | flops | bytes accessed | tf_op | source)
XLA Modules:
  0.0 142.7 jit_solution(14691894582306795041)
XLA Ops:
  0.0 1.1 fusion.193
  1.2 2.6 %collective-permute-start.1 = (f32[16,3,512]{2,1,0:T(4,128)S(1)}, f32[16,3,512]{2,1,0:T(4,128)S(1)}, u32[]{:S(2)}, u32[]{:S(2)}) collective-permute-start(f32[16,3,512]{2,1,0:T(4,128)S(1)} %get-tuple-element.36), channel_id=1, source_target_pairs={{1,0},{2,1},{3,2},{4,3},{5,4},{6,5},{7,6},{8,7},{9,8},{10,9},{11,1... | collective-permute-start | bytes 294920 | tf_op jit(solution)/shard_map/ppermute | solution.py:18
  3.7 3.9 %collective-permute-start = (f32[16,3,512]{2,1,0:T(4,128)S(1)}, f32[16,3,512]{2,1,0:T(4,128)S(1)}, u32[]{:S(2)}, u32[]{:S(2)}) collective-permute-start(f32[16,3,512]{2,1,0:T(4,128)S(1)} %get-tuple-element.37), channel_id=1, source_target_pairs={{0,1},{1,2},{2,3},{3,4},{4,5},{5,6},{6,7},{7,8},{8,9},{9,10},{10,1... | collective-permute-start | bytes 294920 | tf_op jit(solution)/shard_map/ppermute | solution.py:17
  7.8 0.6 collective-permute-done.1
  8.4 1.1 collective-permute-done
  9.8 0.5 fusion.66
  10.3 6.2 %psum.7 = f32[8,512]{1,0:T(8,128)S(1)} all-reduce(f32[8,512]{1,0:T(8,128)S(1)} %get-tuple-element.5), channel_id=1, replica_groups=mesh['tm'=2,'space'=16] {'tm'}, use_global_device_ids=true, to_apply=%region_1.2 | all-reduce | flops 4096 | bytes 32768 | tf_op jit(solution)/shard_map/psum | solution.py:67
  16.5 0.7 pad_maximum_fusion.31
  17.2 3.4 %all-to-all-start = ((bf16[2,16,8,256]{3,2,1,0:T(8,128)(2,1)}), bf16[2,16,8,256]{3,2,1,0:T(8,128)(2,1)S(1)}, u32[]{:S(2)}, u32[]{:S(2)}) async-start(bf16[2,16,8,256]{3,2,1,0:T(8,128)(2,1)} %pad_maximum_fusion.31), calls=%async_computation | async-start | bytes 262144 | tf_op jit(solution)/shard_map/all_to_all | solution.py:70
  20.7 3.3 %all-to-all-done = bf16[2,16,8,256]{3,2,1,0:T(8,128)(2,1)S(1)} async-done(((bf16[2,16,8,256]{3,2,1,0:T(8,128)(2,1)}), bf16[2,16,8,256]{3,2,1,0:T(8,128)(2,1)S(1)}, u32[]{:S(2)}, u32[]{:S(2)}) %all-to-all-start) | async-done | bytes 131104 | tf_op jit(solution)/shard_map/all_to_all | solution.py:70
  24.0 1.9 %collective-permute-start.2 = (bf16[32,8,1]{2,0,1:T(8,128)(2,1)S(1)}, bf16[32,8,1]{2,0,1:T(8,128)(2,1)S(1)}, u32[]{:S(2)}, u32[]{:S(2)}) collective-permute-start(bf16[32,8,1]{2,0,1:T(8,128)(2,1)S(1)} %get-tuple-element.48), channel_id=1, source_target_pairs={{0,16},{1,17},{2,18},{3,19},{4,20},{5,21},{6,22},{7,23},{8,24},{9,... | collective-permute-start | bytes 1544 | tf_op jit(solution)/shard_map/ppermute | solution.py:17
  26.0 1.3 collective-permute-start.3
  27.5 3.4 %collective-permute-done.3 = bf16[32,8,1]{2,0,1:T(8,128)(2,1)S(1)} collective-permute-done((bf16[32,8,1]{2,0,1:T(8,128)(2,1)S(1)}, bf16[32,8,1]{2,0,1:T(8,128)(2,1)S(1)}, u32[]{:S(2)}, u32[]{:S(2)}) %collective-permute-start.3) | collective-permute-done | bytes 544 | tf_op jit(solution)/shard_map/ppermute | solution.py:18
  31.1 10.2 %collective-permute-start.4 = (bf16[32,1,258]{2,0,1:T(8,128)(2,1)S(1)}, bf16[32,1,258]{2,0,1:T(8,128)(2,1)S(1)}, u32[]{:S(2)}, u32[]{:S(2)}) collective-permute-start(bf16[32,1,258]{2,0,1:T(8,128)(2,1)S(1)} %get-tuple-element.34), channel_id=1, source_target_pairs={{0,1},{1,2},{2,3},{3,4},{4,5},{5,6},{6,7},{7,8},{8,9},{9,10},{10,1... | collective-permute-start | bytes 49544 | tf_op jit(solution)/shard_map/ppermute | solution.py:17
  41.2 1.9 %collective-permute-start.5 = (bf16[32,1,258]{2,0,1:T(8,128)(2,1)S(1)}, bf16[32,1,258]{2,0,1:T(8,128)(2,1)S(1)}, u32[]{:S(2)}, u32[]{:S(2)}) collective-permute-start(bf16[32,1,258]{2,0,1:T(8,128)(2,1)S(1)} %get-tuple-element.35), channel_id=1, source_target_pairs={{1,0},{2,1},{3,2},{4,3},{5,4},{6,5},{7,6},{8,7},{9,8},{10,9},{11,1... | collective-permute-start | bytes 49544 | tf_op jit(solution)/shard_map/ppermute | solution.py:18
  43.5 3.8 %collective-permute-done.5 = bf16[32,1,258]{2,0,1:T(8,128)(2,1)S(1)} collective-permute-done((bf16[32,1,258]{2,0,1:T(8,128)(2,1)S(1)}, bf16[32,1,258]{2,0,1:T(8,128)(2,1)S(1)}, u32[]{:S(2)}, u32[]{:S(2)}) %collective-permute-start.5) | collective-permute-done | bytes 16544 | tf_op jit(solution)/shard_map/ppermute | solution.py:18
  49.2 0.3 fusion.51
  49.6 1.3 collective-permute-start.6
  50.9 1.3 collective-permute-start.7
  52.5 3.7 %collective-permute-done.7 = bf16[48,8,1]{2,0,1:T(8,128)(2,1)S(1)} collective-permute-done((bf16[48,8,1]{2,0,1:T(8,128)(2,1)S(1)}, bf16[48,8,1]{2,0,1:T(8,128)(2,1)S(1)}, u32[]{:S(2)}, u32[]{:S(2)}) %collective-permute-start.7) | collective-permute-done | bytes 800 | tf_op jit(solution)/shard_map/ppermute | solution.py:18
  56.4 3.4 %collective-permute-start.8 = (bf16[48,1,258]{2,0,1:T(8,128)(2,1)S(1)}, bf16[48,1,258]{2,0,1:T(8,128)(2,1)S(1)}, u32[]{:S(2)}, u32[]{:S(2)}) collective-permute-start(bf16[48,1,258]{2,0,1:T(8,128)(2,1)S(1)} %get-tuple-element.30), channel_id=1, source_target_pairs={{0,1},{1,2},{2,3},{3,4},{4,5},{5,6},{6,7},{7,8},{8,9},{9,10},{10,1... | collective-permute-start | bytes 74312 | tf_op jit(solution)/shard_map/ppermute | solution.py:17
  59.7 1.9 %collective-permute-start.9 = (bf16[48,1,258]{2,0,1:T(8,128)(2,1)S(1)}, bf16[48,1,258]{2,0,1:T(8,128)(2,1)S(1)}, u32[]{:S(2)}, u32[]{:S(2)}) collective-permute-start(bf16[48,1,258]{2,0,1:T(8,128)(2,1)S(1)} %get-tuple-element.31), channel_id=1, source_target_pairs={{1,0},{2,1},{3,2},{4,3},{5,4},{6,5},{7,6},{8,7},{9,8},{10,9},{11,1... | collective-permute-start | bytes 74312 | tf_op jit(solution)/shard_map/ppermute | solution.py:18
  62.0 4.0 %collective-permute-done.9 = bf16[48,1,258]{2,0,1:T(8,128)(2,1)S(1)} collective-permute-done((bf16[48,1,258]{2,0,1:T(8,128)(2,1)S(1)}, bf16[48,1,258]{2,0,1:T(8,128)(2,1)S(1)}, u32[]{:S(2)}, u32[]{:S(2)}) %collective-permute-start.9) | collective-permute-done | bytes 24800 | tf_op jit(solution)/shard_map/ppermute | solution.py:18
  68.1 1.3 collective-permute-start.10
  69.4 1.3 collective-permute-start.11
  71.0 3.7 %collective-permute-done.11 = bf16[48,8,1]{2,0,1:T(8,128)(2,1)S(1)} collective-permute-done((bf16[48,8,1]{2,0,1:T(8,128)(2,1)S(1)}, bf16[48,8,1]{2,0,1:T(8,128)(2,1)S(1)}, u32[]{:S(2)}, u32[]{:S(2)}) %collective-permute-start.11) | collective-permute-done | bytes 800 | tf_op jit(solution)/shard_map/ppermute | solution.py:18
  74.9 3.3 %collective-permute-start.12 = (bf16[48,1,258]{2,0,1:T(8,128)(2,1)S(1)}, bf16[48,1,258]{2,0,1:T(8,128)(2,1)S(1)}, u32[]{:S(2)}, u32[]{:S(2)}) collective-permute-start(bf16[48,1,258]{2,0,1:T(8,128)(2,1)S(1)} %get-tuple-element.26), channel_id=1, source_target_pairs={{0,1},{1,2},{2,3},{3,4},{4,5},{5,6},{6,7},{7,8},{8,9},{9,10},{10,1... | collective-permute-start | bytes 74312 | tf_op jit(solution)/shard_map/ppermute | solution.py:17
  78.2 1.9 %collective-permute-start.13 = (bf16[48,1,258]{2,0,1:T(8,128)(2,1)S(1)}, bf16[48,1,258]{2,0,1:T(8,128)(2,1)S(1)}, u32[]{:S(2)}, u32[]{:S(2)}) collective-permute-start(bf16[48,1,258]{2,0,1:T(8,128)(2,1)S(1)} %get-tuple-element.27), channel_id=1, source_target_pairs={{1,0},{2,1},{3,2},{4,3},{5,4},{6,5},{7,6},{8,7},{9,8},{10,9},{11,1... | collective-permute-start | bytes 74312 | tf_op jit(solution)/shard_map/ppermute | solution.py:18
  80.4 4.0 %collective-permute-done.13 = bf16[48,1,258]{2,0,1:T(8,128)(2,1)S(1)} collective-permute-done((bf16[48,1,258]{2,0,1:T(8,128)(2,1)S(1)}, bf16[48,1,258]{2,0,1:T(8,128)(2,1)S(1)}, u32[]{:S(2)}, u32[]{:S(2)}) %collective-permute-start.13) | collective-permute-done | bytes 24800 | tf_op jit(solution)/shard_map/ppermute | solution.py:18
  86.6 1.3 collective-permute-start.14
  87.9 1.3 collective-permute-start.15
  89.5 3.7 %collective-permute-done.15 = bf16[48,8,1]{2,0,1:T(8,128)(2,1)S(1)} collective-permute-done((bf16[48,8,1]{2,0,1:T(8,128)(2,1)S(1)}, bf16[48,8,1]{2,0,1:T(8,128)(2,1)S(1)}, u32[]{:S(2)}, u32[]{:S(2)}) %collective-permute-start.15) | collective-permute-done | bytes 800 | tf_op jit(solution)/shard_map/ppermute | solution.py:18
  93.3 3.3 %collective-permute-start.16 = (bf16[48,1,258]{2,0,1:T(8,128)(2,1)S(1)}, bf16[48,1,258]{2,0,1:T(8,128)(2,1)S(1)}, u32[]{:S(2)}, u32[]{:S(2)}) collective-permute-start(bf16[48,1,258]{2,0,1:T(8,128)(2,1)S(1)} %get-tuple-element.22), channel_id=1, source_target_pairs={{0,1},{1,2},{2,3},{3,4},{4,5},{5,6},{6,7},{7,8},{8,9},{9,10},{10,1... | collective-permute-start | bytes 74312 | tf_op jit(solution)/shard_map/ppermute | solution.py:17
  96.6 1.9 %collective-permute-start.17 = (bf16[48,1,258]{2,0,1:T(8,128)(2,1)S(1)}, bf16[48,1,258]{2,0,1:T(8,128)(2,1)S(1)}, u32[]{:S(2)}, u32[]{:S(2)}) collective-permute-start(bf16[48,1,258]{2,0,1:T(8,128)(2,1)S(1)} %get-tuple-element.23), channel_id=1, source_target_pairs={{1,0},{2,1},{3,2},{4,3},{5,4},{6,5},{7,6},{8,7},{9,8},{10,9},{11,1... | collective-permute-start | bytes 74312 | tf_op jit(solution)/shard_map/ppermute | solution.py:18
  98.8 4.0 %collective-permute-done.17 = bf16[48,1,258]{2,0,1:T(8,128)(2,1)S(1)} collective-permute-done((bf16[48,1,258]{2,0,1:T(8,128)(2,1)S(1)}, bf16[48,1,258]{2,0,1:T(8,128)(2,1)S(1)}, u32[]{:S(2)}, u32[]{:S(2)}) %collective-permute-start.17) | collective-permute-done | bytes 24800 | tf_op jit(solution)/shard_map/ppermute | solution.py:18
  105.0 1.3 collective-permute-start.18
  106.3 1.3 collective-permute-start.19
  107.9 3.7 %collective-permute-done.19 = bf16[48,8,1]{2,0,1:T(8,128)(2,1)S(1)} collective-permute-done((bf16[48,8,1]{2,0,1:T(8,128)(2,1)S(1)}, bf16[48,8,1]{2,0,1:T(8,128)(2,1)S(1)}, u32[]{:S(2)}, u32[]{:S(2)}) %collective-permute-start.19) | collective-permute-done | bytes 800 | tf_op jit(solution)/shard_map/ppermute | solution.py:18
  111.8 3.3 %collective-permute-start.20 = (bf16[48,1,258]{2,0,1:T(8,128)(2,1)S(1)}, bf16[48,1,258]{2,0,1:T(8,128)(2,1)S(1)}, u32[]{:S(2)}, u32[]{:S(2)}) collective-permute-start(bf16[48,1,258]{2,0,1:T(8,128)(2,1)S(1)} %get-tuple-element.18), channel_id=1, source_target_pairs={{0,1},{1,2},{2,3},{3,4},{4,5},{5,6},{6,7},{7,8},{8,9},{9,10},{10,1... | collective-permute-start | bytes 74312 | tf_op jit(solution)/shard_map/ppermute | solution.py:17
  115.1 1.9 %collective-permute-start.21 = (bf16[48,1,258]{2,0,1:T(8,128)(2,1)S(1)}, bf16[48,1,258]{2,0,1:T(8,128)(2,1)S(1)}, u32[]{:S(2)}, u32[]{:S(2)}) collective-permute-start(bf16[48,1,258]{2,0,1:T(8,128)(2,1)S(1)} %get-tuple-element.19), channel_id=1, source_target_pairs={{1,0},{2,1},{3,2},{4,3},{5,4},{6,5},{7,6},{8,7},{9,8},{10,9},{11,1... | collective-permute-start | bytes 74312 | tf_op jit(solution)/shard_map/ppermute | solution.py:18
  117.3 4.0 %collective-permute-done.21 = bf16[48,1,258]{2,0,1:T(8,128)(2,1)S(1)} collective-permute-done((bf16[48,1,258]{2,0,1:T(8,128)(2,1)S(1)}, bf16[48,1,258]{2,0,1:T(8,128)(2,1)S(1)}, u32[]{:S(2)}, u32[]{:S(2)}) %collective-permute-start.21) | collective-permute-done | bytes 24800 | tf_op jit(solution)/shard_map/ppermute | solution.py:18
  123.4 1.3 collective-permute-start.22
  124.7 1.3 collective-permute-start.23
  126.4 3.7 %collective-permute-done.23 = bf16[48,8,1]{2,0,1:T(8,128)(2,1)S(1)} collective-permute-done((bf16[48,8,1]{2,0,1:T(8,128)(2,1)S(1)}, bf16[48,8,1]{2,0,1:T(8,128)(2,1)S(1)}, u32[]{:S(2)}, u32[]{:S(2)}) %collective-permute-start.23) | collective-permute-done | bytes 800 | tf_op jit(solution)/shard_map/ppermute | solution.py:18
  130.2 3.3 %collective-permute-start.24 = (bf16[48,1,258]{2,0,1:T(8,128)(2,1)S(1)}, bf16[48,1,258]{2,0,1:T(8,128)(2,1)S(1)}, u32[]{:S(2)}, u32[]{:S(2)}) collective-permute-start(bf16[48,1,258]{2,0,1:T(8,128)(2,1)S(1)} %get-tuple-element.14), channel_id=1, source_target_pairs={{0,1},{1,2},{2,3},{3,4},{4,5},{5,6},{6,7},{7,8},{8,9},{9,10},{10,1... | collective-permute-start | bytes 74312 | tf_op jit(solution)/shard_map/ppermute | solution.py:17
  133.5 1.9 %collective-permute-start.25 = (bf16[48,1,258]{2,0,1:T(8,128)(2,1)S(1)}, bf16[48,1,258]{2,0,1:T(8,128)(2,1)S(1)}, u32[]{:S(2)}, u32[]{:S(2)}) collective-permute-start(bf16[48,1,258]{2,0,1:T(8,128)(2,1)S(1)} %get-tuple-element.15), channel_id=1, source_target_pairs={{1,0},{2,1},{3,2},{4,3},{5,4},{6,5},{7,6},{8,7},{9,8},{10,9},{11,1... | collective-permute-start | bytes 74312 | tf_op jit(solution)/shard_map/ppermute | solution.py:18
  135.7 4.0 %collective-permute-done.25 = bf16[48,1,258]{2,0,1:T(8,128)(2,1)S(1)} collective-permute-done((bf16[48,1,258]{2,0,1:T(8,128)(2,1)S(1)}, bf16[48,1,258]{2,0,1:T(8,128)(2,1)S(1)}, u32[]{:S(2)}, u32[]{:S(2)}) %collective-permute-start.25) | collective-permute-done | bytes 24800 | tf_op jit(solution)/shard_map/ppermute | solution.py:18
  141.8 1.0 copy.5
  (100 shorter events, 17.1 us)
Async XLA Ops:
  0.0 7.7 %copy-start = (f32[16,8,512]{2,1,0:T(8,128)S(1)}, f32[16,8,512]{2,1,0:T(8,128)}, u32[]{:S(2)}) copy-start(f32[16,8,512]{2,1,0:T(8,128)} %param.3) | copy-start | bytes 786436
  1.2 7.2 %collective-permute-start.1 = (f32[16,3,512]{2,1,0:T(4,128)S(1)}, f32[16,3,512]{2,1,0:T(4,128)S(1)}, u32[]{:S(2)}, u32[]{:S(2)}) collective-permute-start(f32[16,3,512]{2,1,0:T(4,128)S(1)} %get-tuple-element.36), channel_id=1, source_target_pairs={{1,0},{2,1},{3,2},{4,3},{5,4},{6,5},{7,6},{8,7},{9,8},{10,9},{11,1... | collective-permute-start | bytes 294920 | tf_op jit(solution)/shard_map/ppermute | solution.py:18
  3.7 5.8 %collective-permute-start = (f32[16,3,512]{2,1,0:T(4,128)S(1)}, f32[16,3,512]{2,1,0:T(4,128)S(1)}, u32[]{:S(2)}, u32[]{:S(2)}) collective-permute-start(f32[16,3,512]{2,1,0:T(4,128)S(1)} %get-tuple-element.37), channel_id=1, source_target_pairs={{0,1},{1,2},{2,3},{3,4},{4,5},{5,6},{6,7},{7,8},{8,9},{9,10},{10,1... | collective-permute-start | bytes 294920 | tf_op jit(solution)/shard_map/ppermute | solution.py:17
  16.4 4.2 %copy-start.1 = (bf16[5,3,3,48,48]{4,3,2,1,0:T(8,128)(2,1)S(1)}, bf16[5,3,3,48,48]{4,3,2,1,0:T(8,128)(2,1)}, u32[]{:S(2)}) copy-start(bf16[5,3,3,48,48]{4,3,2,1,0:T(8,128)(2,1)} %param.5) | copy-start | bytes 622084
  17.2 6.7 %all-to-all-start = ((bf16[2,16,8,256]{3,2,1,0:T(8,128)(2,1)}), bf16[2,16,8,256]{3,2,1,0:T(8,128)(2,1)S(1)}, u32[]{:S(2)}, u32[]{:S(2)}) async-start(bf16[2,16,8,256]{3,2,1,0:T(8,128)(2,1)} %pad_maximum_fusion.31), calls=%async_computation | async-start | bytes 262144 | tf_op jit(solution)/shard_map/all_to_all | solution.py:70
  23.9 3.3 %copy-start.2 = (bf16[3,3,48,32]{2,3,1,0:T(8,128)(2,1)S(1)}, bf16[3,3,48,32]{2,3,1,0:T(8,128)(2,1)}, u32[]{:S(2)}) copy-start(bf16[3,3,48,32]{2,3,1,0:T(8,128)(2,1)} %param.4) | copy-start | bytes 82948
  24.0 3.5 %collective-permute-start.2 = (bf16[32,8,1]{2,0,1:T(8,128)(2,1)S(1)}, bf16[32,8,1]{2,0,1:T(8,128)(2,1)S(1)}, u32[]{:S(2)}, u32[]{:S(2)}) collective-permute-start(bf16[32,8,1]{2,0,1:T(8,128)(2,1)S(1)} %get-tuple-element.48), channel_id=1, source_target_pairs={{0,16},{1,17},{2,18},{3,19},{4,20},{5,21},{6,22},{7,23},{8,24},{9,... | collective-permute-start | bytes 1544 | tf_op jit(solution)/shard_map/ppermute | solution.py:17
  26.0 5.0 %collective-permute-start.3 = (bf16[32,8,1]{2,0,1:T(8,128)(2,1)S(1)}, bf16[32,8,1]{2,0,1:T(8,128)(2,1)S(1)}, u32[]{:S(2)}, u32[]{:S(2)}) collective-permute-start(bf16[32,8,1]{2,0,1:T(8,128)(2,1)S(1)} %get-tuple-element.49), channel_id=1, source_target_pairs={{16,0},{17,1},{18,2},{19,3},{20,4},{21,5},{22,6},{23,7},{24,8},{25... | collective-permute-start | bytes 1544 | tf_op jit(solution)/shard_map/ppermute | solution.py:18
  31.1 12.4 %collective-permute-start.4 = (bf16[32,1,258]{2,0,1:T(8,128)(2,1)S(1)}, bf16[32,1,258]{2,0,1:T(8,128)(2,1)S(1)}, u32[]{:S(2)}, u32[]{:S(2)}) collective-permute-start(bf16[32,1,258]{2,0,1:T(8,128)(2,1)S(1)} %get-tuple-element.34), channel_id=1, source_target_pairs={{0,1},{1,2},{2,3},{3,4},{4,5},{5,6},{6,7},{7,8},{8,9},{9,10},{10,1... | collective-permute-start | bytes 49544 | tf_op jit(solution)/shard_map/ppermute | solution.py:17
  41.2 6.0 %collective-permute-start.5 = (bf16[32,1,258]{2,0,1:T(8,128)(2,1)S(1)}, bf16[32,1,258]{2,0,1:T(8,128)(2,1)S(1)}, u32[]{:S(2)}, u32[]{:S(2)}) collective-permute-start(bf16[32,1,258]{2,0,1:T(8,128)(2,1)S(1)} %get-tuple-element.35), channel_id=1, source_target_pairs={{1,0},{2,1},{3,2},{4,3},{5,4},{6,5},{7,6},{8,7},{9,8},{10,9},{11,1... | collective-permute-start | bytes 49544 | tf_op jit(solution)/shard_map/ppermute | solution.py:18
  49.6 2.9 %collective-permute-start.6 = (bf16[48,8,1]{2,0,1:T(8,128)(2,1)S(1)}, bf16[48,8,1]{2,0,1:T(8,128)(2,1)S(1)}, u32[]{:S(2)}, u32[]{:S(2)}) collective-permute-start(bf16[48,8,1]{2,0,1:T(8,128)(2,1)S(1)} %get-tuple-element.46), channel_id=1, source_target_pairs={{0,16},{1,17},{2,18},{3,19},{4,20},{5,21},{6,22},{7,23},{8,24},{9,... | collective-permute-start | bytes 2312 | tf_op jit(solution)/shard_map/ppermute | solution.py:17
  50.9 5.4 %collective-permute-start.7 = (bf16[48,8,1]{2,0,1:T(8,128)(2,1)S(1)}, bf16[48,8,1]{2,0,1:T(8,128)(2,1)S(1)}, u32[]{:S(2)}, u32[]{:S(2)}) collective-permute-start(bf16[48,8,1]{2,0,1:T(8,128)(2,1)S(1)} %get-tuple-element.47), channel_id=1, source_target_pairs={{16,0},{17,1},{18,2},{19,3},{20,4},{21,5},{22,6},{23,7},{24,8},{25... | collective-permute-start | bytes 2312 | tf_op jit(solution)/shard_map/ppermute | solution.py:18
  56.4 5.6 %collective-permute-start.8 = (bf16[48,1,258]{2,0,1:T(8,128)(2,1)S(1)}, bf16[48,1,258]{2,0,1:T(8,128)(2,1)S(1)}, u32[]{:S(2)}, u32[]{:S(2)}) collective-permute-start(bf16[48,1,258]{2,0,1:T(8,128)(2,1)S(1)} %get-tuple-element.30), channel_id=1, source_target_pairs={{0,1},{1,2},{2,3},{3,4},{4,5},{5,6},{6,7},{7,8},{8,9},{9,10},{10,1... | collective-permute-start | bytes 74312 | tf_op jit(solution)/shard_map/ppermute | solution.py:17
  59.7 6.2 %collective-permute-start.9 = (bf16[48,1,258]{2,0,1:T(8,128)(2,1)S(1)}, bf16[48,1,258]{2,0,1:T(8,128)(2,1)S(1)}, u32[]{:S(2)}, u32[]{:S(2)}) collective-permute-start(bf16[48,1,258]{2,0,1:T(8,128)(2,1)S(1)} %get-tuple-element.31), channel_id=1, source_target_pairs={{1,0},{2,1},{3,2},{4,3},{5,4},{6,5},{7,6},{8,7},{9,8},{10,9},{11,1... | collective-permute-start | bytes 74312 | tf_op jit(solution)/shard_map/ppermute | solution.py:18
  68.1 2.9 %collective-permute-start.10 = (bf16[48,8,1]{2,0,1:T(8,128)(2,1)S(1)}, bf16[48,8,1]{2,0,1:T(8,128)(2,1)S(1)}, u32[]{:S(2)}, u32[]{:S(2)}) collective-permute-start(bf16[48,8,1]{2,0,1:T(8,128)(2,1)S(1)} %get-tuple-element.44), channel_id=1, source_target_pairs={{0,16},{1,17},{2,18},{3,19},{4,20},{5,21},{6,22},{7,23},{8,24},{9,... | collective-permute-start | bytes 2312 | tf_op jit(solution)/shard_map/ppermute | solution.py:17
  69.4 5.4 %collective-permute-start.11 = (bf16[48,8,1]{2,0,1:T(8,128)(2,1)S(1)}, bf16[48,8,1]{2,0,1:T(8,128)(2,1)S(1)}, u32[]{:S(2)}, u32[]{:S(2)}) collective-permute-start(bf16[48,8,1]{2,0,1:T(8,128)(2,1)S(1)} %get-tuple-element.45), channel_id=1, source_target_pairs={{16,0},{17,1},{18,2},{19,3},{20,4},{21,5},{22,6},{23,7},{24,8},{25... | collective-permute-start | bytes 2312 | tf_op jit(solution)/shard_map/ppermute | solution.py:18
  74.9 5.5 %collective-permute-start.12 = (bf16[48,1,258]{2,0,1:T(8,128)(2,1)S(1)}, bf16[48,1,258]{2,0,1:T(8,128)(2,1)S(1)}, u32[]{:S(2)}, u32[]{:S(2)}) collective-permute-start(bf16[48,1,258]{2,0,1:T(8,128)(2,1)S(1)} %get-tuple-element.26), channel_id=1, source_target_pairs={{0,1},{1,2},{2,3},{3,4},{4,5},{5,6},{6,7},{7,8},{8,9},{9,10},{10,1... | collective-permute-start | bytes 74312 | tf_op jit(solution)/shard_map/ppermute | solution.py:17
  78.2 6.2 %collective-permute-start.13 = (bf16[48,1,258]{2,0,1:T(8,128)(2,1)S(1)}, bf16[48,1,258]{2,0,1:T(8,128)(2,1)S(1)}, u32[]{:S(2)}, u32[]{:S(2)}) collective-permute-start(bf16[48,1,258]{2,0,1:T(8,128)(2,1)S(1)} %get-tuple-element.27), channel_id=1, source_target_pairs={{1,0},{2,1},{3,2},{4,3},{5,4},{6,5},{7,6},{8,7},{9,8},{10,9},{11,1... | collective-permute-start | bytes 74312 | tf_op jit(solution)/shard_map/ppermute | solution.py:18
  86.6 2.9 %collective-permute-start.14 = (bf16[48,8,1]{2,0,1:T(8,128)(2,1)S(1)}, bf16[48,8,1]{2,0,1:T(8,128)(2,1)S(1)}, u32[]{:S(2)}, u32[]{:S(2)}) collective-permute-start(bf16[48,8,1]{2,0,1:T(8,128)(2,1)S(1)} %get-tuple-element.42), channel_id=1, source_target_pairs={{0,16},{1,17},{2,18},{3,19},{4,20},{5,21},{6,22},{7,23},{8,24},{9,... | collective-permute-start | bytes 2312 | tf_op jit(solution)/shard_map/ppermute | solution.py:17
  87.9 5.4 %collective-permute-start.15 = (bf16[48,8,1]{2,0,1:T(8,128)(2,1)S(1)}, bf16[48,8,1]{2,0,1:T(8,128)(2,1)S(1)}, u32[]{:S(2)}, u32[]{:S(2)}) collective-permute-start(bf16[48,8,1]{2,0,1:T(8,128)(2,1)S(1)} %get-tuple-element.43), channel_id=1, source_target_pairs={{16,0},{17,1},{18,2},{19,3},{20,4},{21,5},{22,6},{23,7},{24,8},{25... | collective-permute-start | bytes 2312 | tf_op jit(solution)/shard_map/ppermute | solution.py:18
  93.3 5.5 %collective-permute-start.16 = (bf16[48,1,258]{2,0,1:T(8,128)(2,1)S(1)}, bf16[48,1,258]{2,0,1:T(8,128)(2,1)S(1)}, u32[]{:S(2)}, u32[]{:S(2)}) collective-permute-start(bf16[48,1,258]{2,0,1:T(8,128)(2,1)S(1)} %get-tuple-element.22), channel_id=1, source_target_pairs={{0,1},{1,2},{2,3},{3,4},{4,5},{5,6},{6,7},{7,8},{8,9},{9,10},{10,1... | collective-permute-start | bytes 74312 | tf_op jit(solution)/shard_map/ppermute | solution.py:17
  96.6 6.2 %collective-permute-start.17 = (bf16[48,1,258]{2,0,1:T(8,128)(2,1)S(1)}, bf16[48,1,258]{2,0,1:T(8,128)(2,1)S(1)}, u32[]{:S(2)}, u32[]{:S(2)}) collective-permute-start(bf16[48,1,258]{2,0,1:T(8,128)(2,1)S(1)} %get-tuple-element.23), channel_id=1, source_target_pairs={{1,0},{2,1},{3,2},{4,3},{5,4},{6,5},{7,6},{8,7},{9,8},{10,9},{11,1... | collective-permute-start | bytes 74312 | tf_op jit(solution)/shard_map/ppermute | solution.py:18
  105.0 2.9 %collective-permute-start.18 = (bf16[48,8,1]{2,0,1:T(8,128)(2,1)S(1)}, bf16[48,8,1]{2,0,1:T(8,128)(2,1)S(1)}, u32[]{:S(2)}, u32[]{:S(2)}) collective-permute-start(bf16[48,8,1]{2,0,1:T(8,128)(2,1)S(1)} %get-tuple-element.40), channel_id=1, source_target_pairs={{0,16},{1,17},{2,18},{3,19},{4,20},{5,21},{6,22},{7,23},{8,24},{9,... | collective-permute-start | bytes 2312 | tf_op jit(solution)/shard_map/ppermute | solution.py:17
  106.3 5.4 %collective-permute-start.19 = (bf16[48,8,1]{2,0,1:T(8,128)(2,1)S(1)}, bf16[48,8,1]{2,0,1:T(8,128)(2,1)S(1)}, u32[]{:S(2)}, u32[]{:S(2)}) collective-permute-start(bf16[48,8,1]{2,0,1:T(8,128)(2,1)S(1)} %get-tuple-element.41), channel_id=1, source_target_pairs={{16,0},{17,1},{18,2},{19,3},{20,4},{21,5},{22,6},{23,7},{24,8},{25... | collective-permute-start | bytes 2312 | tf_op jit(solution)/shard_map/ppermute | solution.py:18
  111.8 5.5 %collective-permute-start.20 = (bf16[48,1,258]{2,0,1:T(8,128)(2,1)S(1)}, bf16[48,1,258]{2,0,1:T(8,128)(2,1)S(1)}, u32[]{:S(2)}, u32[]{:S(2)}) collective-permute-start(bf16[48,1,258]{2,0,1:T(8,128)(2,1)S(1)} %get-tuple-element.18), channel_id=1, source_target_pairs={{0,1},{1,2},{2,3},{3,4},{4,5},{5,6},{6,7},{7,8},{8,9},{9,10},{10,1... | collective-permute-start | bytes 74312 | tf_op jit(solution)/shard_map/ppermute | solution.py:17
  115.1 6.2 %collective-permute-start.21 = (bf16[48,1,258]{2,0,1:T(8,128)(2,1)S(1)}, bf16[48,1,258]{2,0,1:T(8,128)(2,1)S(1)}, u32[]{:S(2)}, u32[]{:S(2)}) collective-permute-start(bf16[48,1,258]{2,0,1:T(8,128)(2,1)S(1)} %get-tuple-element.19), channel_id=1, source_target_pairs={{1,0},{2,1},{3,2},{4,3},{5,4},{6,5},{7,6},{8,7},{9,8},{10,9},{11,1... | collective-permute-start | bytes 74312 | tf_op jit(solution)/shard_map/ppermute | solution.py:18
  123.4 2.9 %collective-permute-start.22 = (bf16[48,8,1]{2,0,1:T(8,128)(2,1)S(1)}, bf16[48,8,1]{2,0,1:T(8,128)(2,1)S(1)}, u32[]{:S(2)}, u32[]{:S(2)}) collective-permute-start(bf16[48,8,1]{2,0,1:T(8,128)(2,1)S(1)} %get-tuple-element.38), channel_id=1, source_target_pairs={{0,16},{1,17},{2,18},{3,19},{4,20},{5,21},{6,22},{7,23},{8,24},{9,... | collective-permute-start | bytes 2312 | tf_op jit(solution)/shard_map/ppermute | solution.py:17
  124.7 5.4 %collective-permute-start.23 = (bf16[48,8,1]{2,0,1:T(8,128)(2,1)S(1)}, bf16[48,8,1]{2,0,1:T(8,128)(2,1)S(1)}, u32[]{:S(2)}, u32[]{:S(2)}) collective-permute-start(bf16[48,8,1]{2,0,1:T(8,128)(2,1)S(1)} %get-tuple-element.39), channel_id=1, source_target_pairs={{16,0},{17,1},{18,2},{19,3},{20,4},{21,5},{22,6},{23,7},{24,8},{25... | collective-permute-start | bytes 2312 | tf_op jit(solution)/shard_map/ppermute | solution.py:18
  130.2 5.5 %collective-permute-start.24 = (bf16[48,1,258]{2,0,1:T(8,128)(2,1)S(1)}, bf16[48,1,258]{2,0,1:T(8,128)(2,1)S(1)}, u32[]{:S(2)}, u32[]{:S(2)}) collective-permute-start(bf16[48,1,258]{2,0,1:T(8,128)(2,1)S(1)} %get-tuple-element.14), channel_id=1, source_target_pairs={{0,1},{1,2},{2,3},{3,4},{4,5},{5,6},{6,7},{7,8},{8,9},{9,10},{10,1... | collective-permute-start | bytes 74312 | tf_op jit(solution)/shard_map/ppermute | solution.py:17
  133.5 6.2 %collective-permute-start.25 = (bf16[48,1,258]{2,0,1:T(8,128)(2,1)S(1)}, bf16[48,1,258]{2,0,1:T(8,128)(2,1)S(1)}, u32[]{:S(2)}, u32[]{:S(2)}) collective-permute-start(bf16[48,1,258]{2,0,1:T(8,128)(2,1)S(1)} %get-tuple-element.15), channel_id=1, source_target_pairs={{1,0},{2,1},{3,2},{4,3},{5,4},{6,5},{7,6},{8,7},{9,8},{10,9},{11,1... | collective-permute-start | bytes 74312 | tf_op jit(solution)/shard_map/ppermute | solution.py:18
